TPU v7x, 32 devices: a whole 2x2x4 slice. The times are simulated.
32 devices in a mesh: dp: 8 (over z, y), tensor: 4 (over x, core).
Axes of the slice: x: 2, y: 2, z: 4, core: 2. Of those that a mesh axis runs over, the one named last changes fastest.
Arguments:
- tokens: bfloat16 [18688, 1024], P(('dp', 'tensor')), may hold values from -6 to 6
- cotangent: bfloat16 [18688, 1024], P(('dp', 'tensor')), may hold values from -6 to 6
- image_mask: int32 [32], P('dp'), may hold values 0 or 1
- norm_gains: bfloat16 [2, 1024], P(None, 'dp'), may hold values from 0.25 to 1.75
- norm_shifts: bfloat16 [4, 1024], P(None, 'dp'), may hold values from -1.796875 to 1.796875
- w_qkv: bfloat16 [3, 1024, 1024], P(None, 'dp', 'tensor'), may hold values from -0.25 to 0.25
- b_qv: bfloat16 [2, 1024], P(None, ('tensor', 'dp')), may hold values from -3 to 3
- w_out: bfloat16 [1024, 1024], P('tensor', 'dp'), may hold values from -0.4375 to 0.4375
- w_up: bfloat16 [1024, 4096], P('dp', 'tensor'), may hold values from -0.1875 to 0.1875
- up_bias: bfloat16 [4096], P(('tensor', 'dp')), may hold values from -3 to 3
- w_down: bfloat16 [4096, 1024], P('tensor', 'dp'), may hold values from -0.125 to 0.125
Outputs:
- layer_out: bfloat16 [18688, 1024], P(('dp', 'tensor'))
- grad_tokens: bfloat16 [18688, 1024], P(('dp', 'tensor'))
- grad_norm_gains: float32 [2, 1024], P(None, ('dp', 'tensor'))
- grad_norm_shifts: float32 [4, 1024], P(None, ('dp', 'tensor'))
- grad_w_qkv: float32 [3, 1024, 1024], P(None, 'dp', 'tensor')
- grad_b_qv: float32 [2, 1024], P(None, ('tensor', 'dp'))
- grad_w_out: float32 [1024, 1024], P('tensor', 'dp')
- grad_w_up: float32 [1024, 4096], P('dp', 'tensor')
- grad_up_bias: float32 [4096], P(('tensor', 'dp'))
- grad_w_down: float32 [4096, 1024], P('tensor', 'dp')
All inputs are finite; a program needn't handle non-finite values. No bound on the sum of `image_mask` on one device may be relied on, other than what follows from the above.
Results may differ from a plain program's by a relative error of at most 0.02.
Values may be sent and summed in bfloat16 or wider, within the bound.
No kernel may reach another device: no remote copies, remote signals or barrier semaphores. Data moves between devices by JAX's collectives and lax.ppermute only.
A program may use at most 320 MiB of HBM per device.

v0:
```python
import jax
import jax.numpy as jnp
from jax import lax
from jax.sharding import PartitionSpec as P

HEAD_DIM = 64
VALID = 577
SEQ = 584


def layer_norm(rows_in, gain_row, shift_row):
    center = rows_in - jnp.mean(rows_in, axis=1, keepdims=True)
    inverse = lax.rsqrt(jnp.mean(center * center, axis=1, keepdims=True) + 1e-05)
    scaled = center * inverse
    return (scaled, inverse, scaled * gain_row + shift_row)


def norm_back(grad_norm, scaled, inverse, gain_row):
    grad_hat = grad_norm * gain_row
    first_mean = jnp.mean(grad_hat, axis=1, keepdims=True)
    second_mean = jnp.mean(grad_hat * scaled, axis=1, keepdims=True)
    return inverse * (grad_hat - first_mean - scaled * second_mean)


def per_device(
    tokens,
    cotangent,
    image_mask,
    norm_gains,
    norm_shifts,
    w_qkv,
    b_qv,
    w_out,
    w_up,
    up_bias,
    w_down,
):
    tensor_pos = lax.axis_index("tensor")
    local_rows = tokens.shape[0]
    images_dp = image_mask.shape[0]
    score_scale = HEAD_DIM ** (-0.5)
    qkv_full, out_full, bias_full, gains_full, shifts_full = (
        lax.all_gather(w_qkv, "dp", axis=1, tiled=True),
        lax.all_gather(w_out, "dp", axis=1, tiled=True),
        lax.all_gather(b_qv, "dp", axis=1, tiled=True),
        lax.all_gather(norm_gains, "dp", axis=1, tiled=True),
        lax.all_gather(norm_shifts, "dp", axis=1, tiled=True),
    )
    up_full, down_full, cup_full = (
        lax.all_gather(w_up, "dp", axis=0, tiled=True),
        lax.all_gather(w_down, "dp", axis=1, tiled=True),
        lax.all_gather(up_bias, "dp", axis=0, tiled=True),
    )
    gains = gains_full.astype(jnp.float32)
    shifts = shifts_full.astype(jnp.float32)
    width_here = qkv_full.shape[2]
    heads_here = width_here // HEAD_DIM
    owner_image = (tensor_pos * local_rows + lax.iota(jnp.int32, local_rows)) // SEQ
    row_keep = jnp.sum(
        jnp.where(
            owner_image[:, None] == lax.iota(jnp.int32, images_dp)[None, :], image_mask[None, :], 0
        ),
        axis=1,
    ).astype(jnp.float32)[:, None]
    rows_in = tokens.astype(jnp.float32)
    hat_one, inv_one, normed_one = layer_norm(rows_in, gains[0], shifts[0])
    low_one = normed_one.astype(jnp.bfloat16)
    full_one = lax.all_gather(low_one, "tensor", axis=0, tiled=True)
    work_rows = full_one.shape[0]
    head_shape = (work_rows // SEQ, SEQ, heads_here, HEAD_DIM)
    projected = jnp.einsum("rd,cde->cre", full_one, qkv_full, preferred_element_type=jnp.float32)
    bias_wide = bias_full.astype(jnp.float32)
    queries = (projected[0] + bias_wide[0]).astype(jnp.bfloat16).reshape(head_shape)
    keys_all = projected[1].astype(jnp.bfloat16).reshape(head_shape)
    values = (projected[2] + bias_wide[1]).astype(jnp.bfloat16).reshape(head_shape)
    valid_keys = lax.iota(jnp.int32, SEQ) < VALID

    def scores_of(query_blk, key_blk):
        raw_scores = (
            jnp.einsum("qhd,khd->hqk", query_blk, key_blk, preferred_element_type=jnp.float32)
            * score_scale
        )
        return jnp.where(valid_keys[None, None, :], raw_scores, -1e30)

    def attend(blocks):
        query_blk, key_blk, value_blk = blocks
        scores = scores_of(query_blk, key_blk)
        row_max = jnp.max(scores, axis=2, keepdims=True)
        exponent = jnp.exp(scores - row_max)
        row_total = jnp.sum(exponent, axis=2, keepdims=True)
        attn_probs = (exponent / row_total).astype(jnp.bfloat16)
        result = jnp.einsum(
            "hqk,khd->qhd", attn_probs, value_blk, preferred_element_type=jnp.float32
        )
        return (result.astype(jnp.bfloat16), (row_max + jnp.log(row_total))[:, :, 0])

    attended, log_total = lax.map(attend, (queries, keys_all, values))
    flat_out = attended.reshape(work_rows, width_here)
    attn_part = jnp.dot(flat_out, out_full, preferred_element_type=jnp.float32)
    attn_sum = lax.psum_scatter(
        attn_part.astype(jnp.bfloat16), "tensor", scatter_dimension=0, tiled=True
    ).astype(jnp.float32)
    middle = rows_in + row_keep * (attn_sum + shifts[2])
    hat_two, inv_two, normed_two = layer_norm(middle, gains[1], shifts[1])
    low_two = normed_two.astype(jnp.bfloat16)
    full_two = lax.all_gather(low_two, "tensor", axis=0, tiled=True)
    hidden_pre = jnp.dot(full_two, up_full, preferred_element_type=jnp.float32) + cup_full.astype(
        jnp.float32
    )
    gating = jax.nn.sigmoid(1.702 * hidden_pre)
    activated = (hidden_pre * gating).astype(jnp.bfloat16)
    mlp_part = jnp.dot(activated, down_full, preferred_element_type=jnp.float32)
    mlp_sum = lax.psum_scatter(
        mlp_part.astype(jnp.bfloat16), "tensor", scatter_dimension=0, tiled=True
    ).astype(jnp.float32)
    layer_out = (middle + row_keep * (mlp_sum + shifts[3])).astype(jnp.bfloat16)
    grad_top = cotangent.astype(jnp.float32)
    grad_mlp = row_keep * grad_top
    send_mlp = grad_mlp.astype(jnp.bfloat16)
    mlp_grad_full = lax.all_gather(send_mlp, "tensor", axis=0, tiled=True)
    grad_act = jnp.einsum("rd,fd->rf", mlp_grad_full, down_full, preferred_element_type=jnp.float32)
    grad_pre = grad_act * (gating + 1.702 * hidden_pre * gating * (1.0 - gating))
    low_pre = grad_pre.astype(jnp.bfloat16)
    grad_down = jnp.einsum(
        "rf,rd->fd", activated, mlp_grad_full, preferred_element_type=jnp.float32
    )
    grad_up = jnp.einsum("rd,rf->df", full_two, low_pre, preferred_element_type=jnp.float32)
    grad_cup = jnp.sum(grad_pre, axis=0)
    two_part = jnp.einsum("rf,df->rd", low_pre, up_full, preferred_element_type=jnp.float32)
    grad_two = lax.psum_scatter(
        two_part.astype(jnp.bfloat16), "tensor", scatter_dimension=0, tiled=True
    ).astype(jnp.float32)
    grad_mid = grad_top + norm_back(grad_two, hat_two, inv_two, gains[1])
    grad_attn = row_keep * grad_mid
    send_attn = grad_attn.astype(jnp.bfloat16)
    attn_grad_full = lax.all_gather(send_attn, "tensor", axis=0, tiled=True)
    grad_flat = jnp.einsum(
        "rd,ed->re", attn_grad_full, out_full, preferred_element_type=jnp.float32
    ).astype(jnp.bfloat16)
    grad_wout = jnp.einsum(
        "re,rd->ed", flat_out, attn_grad_full, preferred_element_type=jnp.float32
    )
    grad_heads = grad_flat.reshape(head_shape)

    def attend_back(blocks):
        query_blk, key_blk, value_blk, grad_blk, log_blk = blocks
        attn_probs = jnp.exp(scores_of(query_blk, key_blk) - log_blk[:, :, None])
        grad_probs = jnp.einsum(
            "qhd,khd->hqk", grad_blk, value_blk, preferred_element_type=jnp.float32
        )
        row_dot = jnp.sum(attn_probs * grad_probs, axis=2, keepdims=True)
        grad_scores = (attn_probs * (grad_probs - row_dot)).astype(jnp.bfloat16)
        grad_q = (
            jnp.einsum("hqk,khd->qhd", grad_scores, key_blk, preferred_element_type=jnp.float32)
            * score_scale
        )
        grad_k = (
            jnp.einsum("hqk,qhd->khd", grad_scores, query_blk, preferred_element_type=jnp.float32)
            * score_scale
        )
        grad_v = jnp.einsum(
            "hqk,qhd->khd",
            attn_probs.astype(jnp.bfloat16),
            grad_blk,
            preferred_element_type=jnp.float32,
        )
        return (grad_q, grad_k, grad_v)

    grad_q, grad_k, grad_v = lax.map(
        attend_back, (queries, keys_all, values, grad_heads, log_total)
    )
    grad_proj = jnp.stack([grad_q, grad_k, grad_v]).reshape(3, work_rows, width_here)
    grad_bias_qv = jnp.stack([jnp.sum(grad_proj[0], axis=0), jnp.sum(grad_proj[2], axis=0)])
    low_proj = grad_proj.astype(jnp.bfloat16)
    grad_qkv = jnp.einsum("rd,cre->cde", full_one, low_proj, preferred_element_type=jnp.float32)
    one_part = jnp.einsum("cre,cde->rd", low_proj, qkv_full, preferred_element_type=jnp.float32)
    grad_one = lax.psum_scatter(
        one_part.astype(jnp.bfloat16), "tensor", scatter_dimension=0, tiled=True
    ).astype(jnp.float32)
    grad_in = grad_mid + norm_back(grad_one, hat_one, inv_one, gains[0])
    gain_grads = jnp.stack(
        [jnp.sum(grad_one * hat_one, axis=0), jnp.sum(grad_two * hat_two, axis=0)]
    )
    shift_grads = jnp.stack(
        [
            jnp.sum(grad_one, axis=0),
            jnp.sum(grad_two, axis=0),
            jnp.sum(grad_attn, axis=0),
            jnp.sum(grad_mlp, axis=0),
        ]
    )
    qkv_share, wout_share, bias_share, up_share, down_share, cup_share = (
        lax.psum_scatter(
            grad_qkv.astype(jnp.bfloat16), "dp", scatter_dimension=1, tiled=True
        ).astype(jnp.float32),
        lax.psum_scatter(
            grad_wout.astype(jnp.bfloat16), "dp", scatter_dimension=1, tiled=True
        ).astype(jnp.float32),
        lax.psum_scatter(
            grad_bias_qv.astype(jnp.bfloat16), "dp", scatter_dimension=1, tiled=True
        ).astype(jnp.float32),
        lax.psum_scatter(
            grad_up.astype(jnp.bfloat16), "dp", scatter_dimension=0, tiled=True
        ).astype(jnp.float32),
        lax.psum_scatter(
            grad_down.astype(jnp.bfloat16), "dp", scatter_dimension=1, tiled=True
        ).astype(jnp.float32),
        lax.psum_scatter(
            grad_cup.astype(jnp.bfloat16), "dp", scatter_dimension=0, tiled=True
        ).astype(jnp.float32),
    )
    gain_share, shift_share = (
        lax.psum_scatter(gain_grads, ("dp", "tensor"), scatter_dimension=1, tiled=True),
        lax.psum_scatter(shift_grads, ("dp", "tensor"), scatter_dimension=1, tiled=True),
    )
    return (
        layer_out,
        grad_in.astype(jnp.bfloat16),
        gain_share,
        shift_share,
        qkv_share,
        bias_share,
        wout_share,
        up_share,
        cup_share,
        down_share,
    )


def solution(mesh):
    in_specs = (
        P(("dp", "tensor"), None),
        P(("dp", "tensor"), None),
        P("dp"),
        P(None, "dp"),
        P(None, "dp"),
        P(None, "dp", "tensor"),
        P(None, ("tensor", "dp")),
        P("tensor", "dp"),
        P("dp", "tensor"),
        P(("tensor", "dp")),
        P("tensor", "dp"),
    )
    out_specs = (
        P(("dp", "tensor"), None),
        P(("dp", "tensor"), None),
        P(None, ("dp", "tensor")),
        P(None, ("dp", "tensor")),
        P(None, "dp", "tensor"),
        P(None, ("tensor", "dp")),
        P("tensor", "dp"),
        P("dp", "tensor"),
        P(("tensor", "dp")),
        P("tensor", "dp"),
    )
    return jax.shard_map(
        per_device, mesh=mesh, in_specs=in_specs, out_specs=out_specs, check_vma=False
    )
```

profile of v0, /device:TPU:0, one launch (start us, length us, event | category | flops | bytes accessed | tf_op | source)
XLA Modules:
  0.0 1240.6 jit_solution(2609150840192611639)
XLA Ops:
  8.0 22.4 %all_gather.36 = bf16[2,1024]{1,0:T(2,128)(2,1)S(1)} all-gather(bf16[2,128]{1,0:T(2,128)(2,1)} %param.18), channel_id=1, replica_groups=mesh['dp'=8,'tensor'=4] {'dp'}, dimensions={1}, use_global_device_ids=true | all-gather | bytes 4608 | tf_op jit(solution)/shard_map/all_gather | solution.py:46
  30.3 16.6 %all_gather.37 = bf16[4,1024]{1,0:T(4,128)(2,1)S(1)} all-gather(bf16[4,128]{1,0:T(4,128)(2,1)} %param.19), channel_id=1, replica_groups=mesh['dp'=8,'tensor'=4] {'dp'}, dimensions={1}, use_global_device_ids=true | all-gather | bytes 9216 | tf_op jit(solution)/shard_map/all_gather | solution.py:47
  52.5 18.1 %all-gather = bf16[8,32,2]{1,2,0:T(2,128)(2,1)S(1)} all-gather(bf16[1,32,2]{1,2,0:T(2,128)(2,1)S(1)} %bitcast.216), channel_id=1, replica_groups=mesh['dp'=8,'tensor'=4] {'dp'}, dimensions={0}, use_global_device_ids=true | all-gather | bytes 1152 | tf_op jit(solution)/shard_map/all_gather | solution.py:45
  70.9 27.0 %all_gather.41 = bf16[256,1024]{1,0:T(8,128)(2,1)S(1)} all-gather(bf16[256,128]{1,0:T(8,128)(2,1)S(1)} %copy-done.18), channel_id=1, replica_groups=mesh['dp'=8,'tensor'=4] {'dp'}, dimensions={1}, use_global_device_ids=true | all-gather | bytes 589824 | tf_op jit(solution)/shard_map/all_gather | solution.py:44
  97.9 6.2 convolution_bitcast_fusion
  137.5 29.4 %while.28 = (s32[]{:T(128)}, bf16[4,584,4,64]{1,3,2,0:T(8,128)(2,1)}, f32[4,4,584]{2,1,0:T(4,128)S(1)}, bf16[4,584,4,64]{1,3,2,0:T(8,128)(2,1)}, bf16[4,584,4,64...) while((s32[]{:T(128)}, bf16[4,584,4,64]{1,3,2,0:T(8,128)(2,1)}, ...), condition=%wide.region_6.7_spmd.clone, body=%wide.region_3.6_spmd.clone.sunk | while | flops 365759776 | bytes 17763760 | solution.py:97
  180.0 45.5 %reduce-scatter.24.cloned.1.call-done = bf16[584,1024]{1,0:T(8,128)(2,1)} async-done(((bf16[2336,1024]{1,0:T(8,128)(2,1)}), bf16[584,1024]{1,0:T(8,128)(2,1)}) %reduce-scatter.24.cloned.1.call-update) | async-done | bytes 1196048 | tf_op jit(solution)/shard_map/reduce_scatter | solution.py:100
  233.9 20.4 %all-gather.1 = bf16[8,1,128]{2,1,0:T(2,128)(2,1)S(1)} all-gather(bf16[1,1,128]{2,1,0:T(2,128)(2,1)S(1)} %bitcast.217), channel_id=1, replica_groups=mesh['dp'=8,'tensor'=4] {'dp'}, dimensions={0}, use_global_device_ids=true | all-gather | bytes 2304 | tf_op jit(solution)/shard_map/all_gather | solution.py:52
  254.3 22.8 %all-gather.16.cloned.1.call-done = bf16[1024,1024]{1,0:T(8,128)(2,1)} async-done(((bf16[128,1024]{1,0:T(8,128)(2,1)}), bf16[1024,1024]{1,0:T(8,128)(2,1)}) %all-gather.16.cloned.1.call-update) | async-done | bytes 2097168 | tf_op jit(solution)/shard_map/all_gather | solution.py:50
  277.1 38.4 %all-gather.14.cloned.1.call-done = bf16[2336,1024]{1,0:T(8,128)(2,1)} async-done(((bf16[584,1024]{1,0:T(8,128)(2,1)}), bf16[2336,1024]{1,0:T(8,128)(2,1)}) %all-gather.14.cloned.1.call-update) | async-done | bytes 4784144 | tf_op jit(solution)/shard_map/all_gather | solution.py:106
  315.5 12.6 %multiply_convert_fusion.1 = (bf16[2336,1024]{1,0:T(8,128)(2,1)}, f32[2336,1024]{1,0:T(8,128)}) fusion(f32[1024]{0:T(1024)S(1)} %bitcast.214, bf16[2336,1024]{1,0:T(8,128)(2,1)} %all-gather.14.cloned.1.call-done, bf16[1024,1024]{1,0:T(8,128)(2,1)} %all-gather.16.cloned.1.call-done), kind=kOutput, calls=%fused_computation.65 | convolution fusion | flops 4915691520 | bytes 21237760 | tf_op jit(solution)/shard_map/dot_general | solution.py:107
  328.1 40.6 %all-gather.18.cloned.1.call-done = bf16[1024,1024]{1,0:T(8,128)(2,1)} async-done(((bf16[1024,128]{1,0:T(8,128)(2,1)}), bf16[1024,1024]{1,0:T(8,128)(2,1)}) %all-gather.18.cloned.1.call-update) | async-done | bytes 2097168 | tf_op jit(solution)/shard_map/all_gather | solution.py:51
  368.8 38.3 %all-gather.20.cloned.1.call-done = bf16[2336,1024]{1,0:T(8,128)(2,1)} async-done(((bf16[584,1024]{1,0:T(8,128)(2,1)}), bf16[2336,1024]{1,0:T(8,128)(2,1)}) %all-gather.20.cloned.1.call-update) | async-done | bytes 4784144 | tf_op jit(solution)/shard_map/all_gather | solution.py:120
  407.0 12.7 %fusion.105 = (bf16[1024]{0:T(1024)(128)(2,1)S(1)}, bf16[2336,1024]{1,0:T(8,128)(2,1)S(1)}) fusion(f32[2336,1024]{1,0:T(8,128)} %get-tuple-element.329, f32[1024]{0:T(1024)S(1)} %bitcast.215, bf16[2336,1024]{1,0:T(8,128)(2,1)} %all-gather.20.cloned.1.call-done, bf16[1024,1024]{1,0:T(8,128)(2,1)} %all-gather.18.cloned.1.call-done), kind=kOutput, calls=%fused_computation.159 | convolution fusion | flops 4927650816 | bytes 21239808 | tf_op jit(solution)/shard_map/rd,fd->rf/dot_general | solution.py:121
  421.9 6.9 convolution_convert_fusion
  428.9 9.6 convolution_convert_fusion.1
  438.7 38.5 %reduce-scatter.28.cloned.1.call-done = bf16[584,1024]{1,0:T(8,128)(2,1)} async-done(((bf16[2336,1024]{1,0:T(8,128)(2,1)}), bf16[584,1024]{1,0:T(8,128)(2,1)}) %reduce-scatter.28.cloned.1.call-update) | async-done | bytes 1196048 | tf_op jit(solution)/shard_map/reduce_scatter | solution.py:130
  480.7 47.3 %reduce-scatter.26.cloned.1.call-done = bf16[584,1024]{1,0:T(8,128)(2,1)} async-done(((bf16[2336,1024]{1,0:T(8,128)(2,1)}), bf16[584,1024]{1,0:T(8,128)(2,1)}) %reduce-scatter.26.cloned.1.call-update) | async-done | bytes 1196048 | tf_op jit(solution)/shard_map/reduce_scatter | solution.py:113
  535.1 10.0 convolution_convert_fusion.4
  549.1 10.0 fusion.89
  559.4 13.6 %all-gather.22.cloned.1.call-done = bf16[2336,1024]{1,0:T(8,128)(2,1)} async-done(((bf16[584,1024]{1,0:T(8,128)(2,1)}), bf16[2336,1024]{1,0:T(8,128)(2,1)}) %all-gather.22.cloned.1.call-update) | async-done | bytes 4784144 | tf_op jit(solution)/shard_map/all_gather | solution.py:136
  583.3 53.3 %while.29 = (s32[]{:T(128)}, f32[4,584,4,64]{1,3,2,0:T(8,128)}, bf16[4,584,4,64]{1,3,2,0:T(8,128)(2,1)}, f32[4,584,4,64]{1,3,2,0:T(8,128)}, bf16[4,584,4,64]{1,3...) while((s32[]{:T(128)}, f32[4,584,4,64]{1,3,2,0:T(8,128)}, ...), condition=%wide.region_16.17_spmd.clone, body=%wide.region_14.16_spmd.clone.sunk | while | flops 893863936 | bytes 60922836 | solution.py:169
  636.6 5.8 fusion.101
  676.0 9.0 fusion.95
  689.6 8.6 bitcast_convert_fusion
  700.1 21.7 %all-reduce = bf16[1024]{0:T(1024)(128)(2,1)S(1)} all-reduce(bf16[1024]{0:T(1024)(128)(2,1)S(1)} %get-tuple-element.330), channel_id=12, replica_groups=mesh['dp'=8,'tensor'=4] {'dp'}, use_global_device_ids=true, to_apply=%region_35.36.clone | all-reduce | flops 1024 | bytes 4096
  726.1 54.3 %reduce-scatter.40.cloned.1.call-done = bf16[32,2]{1,0:T(8,128)(2,1)} async-done(((bf16[256,2]{1,0:T(8,128)(2,1)}), bf16[32,2]{1,0:T(8,128)(2,1)}) %reduce-scatter.40.cloned.1.call-update) | async-done | bytes 144
  781.7 63.2 %reduce-scatter.42.cloned.1.call-done = bf16[128,256]{1,0:T(8,128)(2,1)} async-done(((bf16[1024,256]{1,0:T(8,128)(2,1)}), bf16[128,256]{1,0:T(8,128)(2,1)}) %reduce-scatter.42.cloned.1.call-update) | async-done | bytes 65552
  846.5 65.7 %reduce-scatter.38.cloned.1.call-done = bf16[128,768]{1,0:T(8,128)(2,1)} async-done(((bf16[1024,768]{1,0:T(8,128)(2,1)}), bf16[128,768]{1,0:T(8,128)(2,1)}) %reduce-scatter.38.cloned.1.call-update) | async-done | bytes 196624
  914.3 47.6 %reduce-scatter.30.cloned.1.call-done = bf16[584,1024]{1,0:T(8,128)(2,1)} async-done(((bf16[2336,1024]{1,0:T(8,128)(2,1)}), bf16[584,1024]{1,0:T(8,128)(2,1)}) %reduce-scatter.30.cloned.1.call-update) | async-done | bytes 1196048 | tf_op jit(solution)/shard_map/reduce_scatter | solution.py:177
  970.3 129.4 %reduce-scatter.34.cloned.1.call-done = f32[32,2]{1,0:T(8,128)} async-done(((f32[1024,2]{1,0:T(8,128)}), f32[32,2]{1,0:T(8,128)}) %reduce-scatter.34.cloned.1.call-update) | async-done | bytes 272
  1101.1 130.8 %reduce-scatter.36.cloned.1.call-done = f32[32,4]{1,0:T(8,128)} async-done(((f32[1024,4]{1,0:T(8,128)}), f32[32,4]{1,0:T(8,128)}) %reduce-scatter.36.cloned.1.call-update) | async-done | bytes 528
  (251 shorter events, 230.4 us)
Async XLA Ops:
  7.2 43.7 %copy-start = (bf16[584,1024]{1,0:T(8,128)(2,1)S(1)}, bf16[584,1024]{1,0:T(8,128)(2,1)}, u32[]{:S(2)}) copy-start(bf16[584,1024]{1,0:T(8,128)(2,1)} %param.15) | copy-start | bytes 3588100
  7.2 90.8 %all-gather.12.cloned.1.call-start = ((), (), s32[]{:S(2)}) async-start(), calls=%async_computation.12 | async-start | bytes 1769472 | tf_op jit(solution)/shard_map/all_gather | solution.py:43
  7.9 90.0 %all-gather.10.cloned.1.call-start = ((), (), s32[]{:S(2)}) async-start(), calls=%async_computation.11 | async-start | bytes 5980160 | tf_op jit(solution)/shard_map/all_gather | solution.py:68
  48.5 4.1 copy-start.20
  48.5 22.4 %copy-start.18 = (bf16[256,128]{1,0:T(8,128)(2,1)S(1)}, bf16[256,128]{1,0:T(8,128)(2,1)}, u32[]{:S(2)}) copy-start(bf16[256,128]{1,0:T(8,128)(2,1)} %param.22) | copy-start | bytes 196612
  52.5 173.1 %reduce-scatter.24.cloned.1.call-start = ((), (), s32[]{:S(2)}) async-start(), calls=%async_computation.13 | async-start | bytes 5980160 | tf_op jit(solution)/shard_map/reduce_scatter | solution.py:100
  167.0 7.4 copy-start.2
  179.3 97.9 %all-gather.16.cloned.1.call-start = ((), (), s32[]{:S(2)}) async-start(), calls=%async_computation.15 | async-start | bytes 2359296 | tf_op jit(solution)/shard_map/all_gather | solution.py:50
  179.8 135.7 %all-gather.14.cloned.1.call-start = ((), (), s32[]{:S(2)}) async-start(), calls=%async_computation.14 | async-start | bytes 5980160 | tf_op jit(solution)/shard_map/all_gather | solution.py:106
  230.7 3.2 copy-start.22
  232.5 136.3 %all-gather.18.cloned.1.call-start = ((), (), s32[]{:S(2)}) async-start(), calls=%async_computation.16 | async-start | bytes 2359296 | tf_op jit(solution)/shard_map/all_gather | solution.py:51
  233.1 173.9 %all-gather.20.cloned.1.call-start = ((), (), s32[]{:S(2)}) async-start(), calls=%async_computation.18 | async-start | bytes 5980160 | tf_op jit(solution)/shard_map/all_gather | solution.py:120
  233.8 243.4 %reduce-scatter.28.cloned.1.call-start = ((), (), s32[]{:S(2)}) async-start(), calls=%async_computation.19 | async-start | bytes 5980160 | tf_op jit(solution)/shard_map/reduce_scatter | solution.py:130
  407.0 14.9 %copy-start.23 = (bf16[1024,1024]{1,0:T(8,128)(2,1)S(1)}, bf16[1024,1024]{1,0:T(8,128)(2,1)}, u32[]{:S(2)}) copy-start(bf16[1024,1024]{1,0:T(8,128)(2,1)} %all-gather.16.cloned.1.call-done) | copy-start | bytes 6291460
  428.8 99.3 %reduce-scatter.26.cloned.1.call-start = ((), (), s32[]{:S(2)}) async-start(), calls=%async_computation.17 | async-start | bytes 5980160 | tf_op jit(solution)/shard_map/reduce_scatter | solution.py:113
  438.4 89.6 %copy-start.19 = (f32[1,1024]{1,0:T(1,128)S(1)}, f32[1,1024]{1,0:T(1,128)}, u32[]{:S(2)}) copy-start(f32[1,1024]{1,0:T(1,128)} %get-tuple-element.320) | copy-start | bytes 12292
  438.5 134.6 %all-gather.22.cloned.1.call-start = ((), (), s32[]{:S(2)}) async-start(), calls=%async_computation.20 | async-start | bytes 5980160 | tf_op jit(solution)/shard_map/all_gather | solution.py:136
  535.0 187.3 %reduce-scatter.44.cloned.1.call-start = ((), (), s32[]{:S(2)}) async-start(), calls=%async_computation.28 | async-start | bytes 2359296
  549.1 175.2 %reduce-scatter.32.cloned.1.call-start = ((), (), s32[]{:S(2)}) async-start(), calls=%async_computation.22 | async-start | bytes 2359296 | tf_op jit(solution)/shard_map/reduce_scatter | solution.py:202
  559.2 221.2 %reduce-scatter.40.cloned.1.call-start = ((), (), s32[]{:S(2)}) async-start(), calls=%async_computation.26 | async-start | bytes 73728
  578.9 4.3 copy-start.3
  646.0 5.0 copy-start.5
  650.7 194.2 %reduce-scatter.42.cloned.1.call-start = ((), (), s32[]{:S(2)}) async-start(), calls=%async_computation.27 | async-start | bytes 589824
  651.0 4.0 copy-start.9
  672.5 239.8 %reduce-scatter.38.cloned.1.call-start = ((), (), s32[]{:S(2)}) async-start(), calls=%async_computation.25 | async-start | bytes 1769472
  689.6 272.4 %reduce-scatter.30.cloned.1.call-start = ((), (), s32[]{:S(2)}) async-start(), calls=%async_computation.21 | async-start | bytes 5980160 | tf_op jit(solution)/shard_map/reduce_scatter | solution.py:177
  698.2 263.8 %copy-start.13 = (f32[584]{0:T(1024)S(1)}, f32[584]{0:T(1024)}, u32[]{:S(2)}) copy-start(f32[584]{0:T(1024)} %copy-done.12) | copy-start | bytes 7012
  698.2 263.8 %copy-start.15 = (f32[584]{0:T(1024)S(1)}, f32[584]{0:T(1024)}, u32[]{:S(2)}) copy-start(f32[584]{0:T(1024)} %copy-done.14) | copy-start | bytes 7012
  698.2 263.7 %copy-start.17 = (f32[1,1024]{1,0:T(1,128)S(1)}, f32[1,1024]{1,0:T(1,128)}, u32[]{:S(2)}) copy-start(f32[1,1024]{1,0:T(1,128)} %copy-done.16) | copy-start | bytes 12292
  698.2 401.5 %reduce-scatter.34.cloned.1.call-start = ((), (), s32[]{:S(2)}) async-start(), calls=%async_computation.23 | async-start | bytes 540672
  962.0 4.8 copy-start.8
  965.6 266.3 %reduce-scatter.36.cloned.1.call-start = ((), (), s32[]{:S(2)}) async-start(), calls=%async_computation.24 | async-start | bytes 540672
  (21 other events, 40.5 us)
Sparse Core Ops, SparseCore 0:
  10.2 46.6 all-gather.11
  59.1 36.6 all-gather.9
  179.4 46.1 reduce-scatter.23
  227.7 49.3 all-gather.15
  279.2 36.3 all-gather.13
  317.6 51.0 all-gather.17
  371.0 35.9 all-gather.19
  428.9 48.2 reduce-scatter.27
  479.8 48.2 reduce-scatter.25
  535.1 37.8 all-gather.21
  577.0 67.9 reduce-scatter.43
  648.8 66.9 reduce-scatter.31
  720.2 60.1 reduce-scatter.39
  784.0 60.8 reduce-scatter.41
  848.2 64.0 reduce-scatter.37
  914.8 47.1 reduce-scatter.29
  965.7 133.9 reduce-scatter.33
  1101.9 129.9 reduce-scatter.35
where the time goes:
time: 1250 us; the launch traced here: 1240 us
  waiting for transfers between devices  779 us (62%)
  matrix products  167 us (13%)
  blocking collectives  126 us (10%)
  local copies, waits for them, and re-layouts  95.9 us (8%)
  other arithmetic  55 us (4%)
  between operations  15.9 us (1%)
    unnamed x24, waiting for transfers between devices  446 us
    reduce_scatter x1, waiting for transfers between devices, per_device(): lax.psum_scatter(one_part.astype(jnp.bfloat16), 'tensor', scatter_dimensi...  47.6 us
    reduce_scatter x1, waiting for transfers between devices, per_device(): lax.psum_scatter(mlp_part.astype(jnp.bfloat16), 'tensor', scatter_dimensi...  47.3 us
    reduce_scatter x1, waiting for transfers between devices, per_device(): lax.psum_scatter(attn_part.astype(jnp.bfloat16), 'tensor', scatter_dimens...  45.5 us
    all_gather x1, waiting for transfers between devices, per_device(): lax.all_gather(w_down, 'dp', axis=1, tiled=True)  40.6 us
    reduce_scatter x1, waiting for transfers between devices, per_device(): lax.psum_scatter(two_part.astype(jnp.bfloat16), 'tensor', scatter_dimensi...  38.5 us
    unnamed x68, local copies, waits for them, and re-layouts  38.5 us
    all_gather x1, waiting for transfers between devices, per_device(): full_two = lax.all_gather(low_two, 'tensor', axis=0, tiled=True)  38.4 us
  transfers between devices with their start and end apart: 18, of which 14 were waited for; matrix products, arithmetic and copies ran while one was open for 16% of the time, Pallas kernels for 0%

commit v1 on v0

--- a/solution.py
+++ b/solution.py
@@ -2,6 +2,7 @@
 import jax.numpy as jnp
 from jax import lax
 from jax.sharding import PartitionSpec as P
+from jax.lax import axis_index, ppermute, psum
 
 HEAD_DIM = 64
 VALID = 577
@@ -103,7 +104,25 @@
     middle = rows_in + row_keep * (attn_sum + shifts[2])
     hat_two, inv_two, normed_two = layer_norm(middle, gains[1], shifts[1])
     low_two = normed_two.astype(jnp.bfloat16)
-    full_two = lax.all_gather(low_two, "tensor", axis=0, tiled=True)
+
+    def produce_the_notes(packet):
+        n_dev_all = psum(1, "tensor")
+        m = 1
+        stack_in = [packet]
+        while m < n_dev_all:
+            stack_in.append(
+                ppermute(
+                    stack_in[m - 1],
+                    "tensor",
+                    [(no, (no - 1) % n_dev_all) for no in range(n_dev_all)],
+                )
+            )
+            m = m + 1
+        parts_out = jnp.concatenate(stack_in, 0)
+        passed = jnp.roll(parts_out, axis_index("tensor") * packet.shape[0], 0)
+        return passed
+
+    full_two = produce_the_notes(low_two)
     hidden_pre = jnp.dot(full_two, up_full, preferred_element_type=jnp.float32) + cup_full.astype(
         jnp.float32
     )

time: 1250 us -> 1210 us (0.968)
  waiting for transfers between devices: 779 us -> 715 us
  local copies, waits for them, and re-layouts: 95.9 us -> 115 us
    all_gather x1 -> x0, waiting for transfers between devices: 38.4 us -> none  [per_device(): full_two = lax.all_gather(low_two, 'tensor', axis=0, tiled=True)]
    ppermute x0 -> x3, waiting for transfers between devices: none -> 27.8 us  [produce_the_notes(): ppermute(stack_in[m - 1], 'tensor', [(no, (no - 1) % n_dev_all) for no in...]
    all_gather x1, waiting for transfers between devices: 40.6 us -> 14.4 us  [per_device(): lax.all_gather(w_down, 'dp', axis=1, tiled=True)]
    all_gather x1, waiting for transfers between devices: 22.8 us -> 0.01 us  [per_device(): lax.all_gather(w_up, 'dp', axis=0, tiled=True)]
    unnamed x68 -> x84, local copies, waits for them, and re-layouts: 38.5 us -> 52.1 us
    unnamed x24 -> x23, waiting for transfers between devices: 446 us -> 442 us
  transfers between devices with their start and end apart: 18 -> 20, of which waited for: 14 -> 14; matrix products, arithmetic and copies ran while one was open for 16% -> 18% of each run, Pallas kernels for 0% -> 0%
where the time goes in v1:
time: 1210 us; the launch traced here: 1200 us
  waiting for transfers between devices  715 us (59%)
  matrix products  167 us (14%)
  blocking collectives  126 us (10%)
  local copies, waits for them, and re-layouts  115 us (10%)
  other arithmetic  55.4 us (5%)
  between operations  15.5 us (1%)
    unnamed x23, waiting for transfers between devices  442 us
    unnamed x84, local copies, waits for them, and re-layouts  52.1 us
    reduce_scatter x1, waiting for transfers between devices, per_device(): lax.psum_scatter(one_part.astype(jnp.bfloat16), 'tensor', scatter_dimensi...  47.6 us
    reduce_scatter x1, waiting for transfers between devices, per_device(): lax.psum_scatter(mlp_part.astype(jnp.bfloat16), 'tensor', scatter_dimensi...  47.3 us
    reduce_scatter x1, waiting for transfers between devices, per_device(): lax.psum_scatter(attn_part.astype(jnp.bfloat16), 'tensor', scatter_dimens...  44.9 us
    reduce_scatter x1, waiting for transfers between devices, per_device(): lax.psum_scatter(two_part.astype(jnp.bfloat16), 'tensor', scatter_dimensi...  38.6 us
    all_gather x1, waiting for transfers between devices, per_device(): mlp_grad_full = lax.all_gather(send_mlp, 'tensor', axis=0, tiled=True)  38.1 us
    ppermute x3, waiting for transfers between devices, produce_the_notes(): ppermute(stack_in[m - 1], 'tensor', [(no, (no - 1) % n_dev_all) for no in...  27.8 us
  transfers between devices with their start and end apart: 20, of which 14 were waited for; matrix products, arithmetic and copies ran while one was open for 18% of the time, Pallas kernels for 0%

profile of v1, /device:TPU:0, one launch (start us, length us, event | category | flops | bytes accessed | tf_op | source)
XLA Modules:
  0.0 1199.9 jit_solution(10703574277996962256)
XLA Ops:
  8.0 22.4 %all_gather.33 = bf16[2,1024]{1,0:T(2,128)(2,1)S(1)} all-gather(bf16[2,128]{1,0:T(2,128)(2,1)} %param.18), channel_id=1, replica_groups=mesh['dp'=8,'tensor'=4] {'dp'}, dimensions={1}, use_global_device_ids=true | all-gather | bytes 4608 | tf_op jit(solution)/shard_map/all_gather | solution.py:47
  30.3 16.6 %all_gather.34 = bf16[4,1024]{1,0:T(4,128)(2,1)S(1)} all-gather(bf16[4,128]{1,0:T(4,128)(2,1)} %param.19), channel_id=1, replica_groups=mesh['dp'=8,'tensor'=4] {'dp'}, dimensions={1}, use_global_device_ids=true | all-gather | bytes 9216 | tf_op jit(solution)/shard_map/all_gather | solution.py:48
  52.5 18.1 %all-gather = bf16[8,32,2]{1,2,0:T(2,128)(2,1)S(1)} all-gather(bf16[1,32,2]{1,2,0:T(2,128)(2,1)S(1)} %bitcast.214), channel_id=1, replica_groups=mesh['dp'=8,'tensor'=4] {'dp'}, dimensions={0}, use_global_device_ids=true | all-gather | bytes 1152 | tf_op jit(solution)/shard_map/all_gather | solution.py:46
  70.9 27.0 %all_gather.38 = bf16[256,1024]{1,0:T(8,128)(2,1)S(1)} all-gather(bf16[256,128]{1,0:T(8,128)(2,1)S(1)} %copy-done.23), channel_id=1, replica_groups=mesh['dp'=8,'tensor'=4] {'dp'}, dimensions={1}, use_global_device_ids=true | all-gather | bytes 589824 | tf_op jit(solution)/shard_map/all_gather | solution.py:45
  97.9 6.2 convolution_bitcast_fusion
  137.6 29.2 %while.28 = (s32[]{:T(128)}, bf16[4,584,4,64]{1,3,2,0:T(8,128)(2,1)}, f32[4,4,584]{2,1,0:T(4,128)S(1)}, bf16[4,584,4,64]{1,3,2,0:T(8,128)(2,1)}, bf16[4,584,4,64...) while((s32[]{:T(128)}, bf16[4,584,4,64]{1,3,2,0:T(8,128)(2,1)}, ...), condition=%wide.region_6.7_spmd.clone, body=%wide.region_3.6_spmd.clone.sunk | while | flops 365759776 | bytes 17763752 | solution.py:98
  180.5 44.9 %reduce-scatter.24.cloned.1.call-done = bf16[584,1024]{1,0:T(8,128)(2,1)} async-done(((bf16[2336,1024]{1,0:T(8,128)(2,1)}), bf16[584,1024]{1,0:T(8,128)(2,1)}) %reduce-scatter.24.cloned.1.call-update) | async-done | bytes 1196048 | tf_op jit(solution)/shard_map/reduce_scatter | solution.py:101
  232.5 13.9 %collective-permute-done = bf16[584,1024]{1,0:T(8,128)(2,1)S(1)} collective-permute-done((bf16[584,1024]{1,0:T(8,128)(2,1)S(1)}, bf16[584,1024]{1,0:T(8,128)(2,1)S(1)}, u32[]{:S(2)}, u32[]{:S(2)}) %collective-permute-start) | collective-permute-done | bytes 1196064 | tf_op jit(solution)/shard_map/ppermute | solution.py:114
  249.7 13.9 %collective-permute-done.1 = bf16[584,1024]{1,0:T(8,128)(2,1)} collective-permute-done((bf16[584,1024]{1,0:T(8,128)(2,1)S(1)}, bf16[584,1024]{1,0:T(8,128)(2,1)}, u32[]{:S(2)}, u32[]{:S(2)}) %collective-permute-start.1) | collective-permute-done | bytes 1196064 | tf_op jit(solution)/shard_map/ppermute | solution.py:114
  265.9 20.4 %all-gather.1 = bf16[8,1,128]{2,1,0:T(2,128)(2,1)S(1)} all-gather(bf16[1,1,128]{2,1,0:T(2,128)(2,1)S(1)} %bitcast.215), channel_id=1, replica_groups=mesh['dp'=8,'tensor'=4] {'dp'}, dimensions={0}, use_global_device_ids=true | all-gather | bytes 2304 | tf_op jit(solution)/shard_map/all_gather | solution.py:53
  300.8 13.4 %multiply_convert_fusion.1 = (bf16[2336,1024]{1,0:T(8,128)(2,1)}, f32[2336,1024]{1,0:T(8,128)}) fusion(f32[1024]{0:T(1024)S(1)} %bitcast.212, bf16[1024,1024]{1,0:T(8,128)(2,1)} %all-gather.13.cloned.1.call-done, bf16[4672,1024]{1,0:T(8,128)(2,1)} %constant_dynamic-update-slice_fusion, s32[]{:T(128)S(6)} %select_n.36), kind=kOutput, calls=%fused_computation.65 | convolution fusion | flops 4915691520 | bytes 21237764 | tf_op jit(solution)/shard_map/dot_general | solution.py:126
  314.2 14.4 %all-gather.15.cloned.1.call-done = bf16[1024,1024]{1,0:T(8,128)(2,1)} async-done(((bf16[1024,128]{1,0:T(8,128)(2,1)}), bf16[1024,1024]{1,0:T(8,128)(2,1)}) %all-gather.15.cloned.1.call-update) | async-done | bytes 2097168 | tf_op jit(solution)/shard_map/all_gather | solution.py:52
  328.6 38.1 %all-gather.17.cloned.1.call-done = bf16[2336,1024]{1,0:T(8,128)(2,1)} async-done(((bf16[584,1024]{1,0:T(8,128)(2,1)}), bf16[2336,1024]{1,0:T(8,128)(2,1)}) %all-gather.17.cloned.1.call-update) | async-done | bytes 4784144 | tf_op jit(solution)/shard_map/all_gather | solution.py:139
  366.8 12.7 %fusion.112 = (bf16[1024]{0:T(1024)(128)(2,1)S(1)}, bf16[2336,1024]{1,0:T(8,128)(2,1)S(1)}) fusion(f32[2336,1024]{1,0:T(8,128)} %get-tuple-element.331, f32[1024]{0:T(1024)S(1)} %bitcast.213, bf16[2336,1024]{1,0:T(8,128)(2,1)} %all-gather.17.cloned.1.call-done, bf16[1024,1024]{1,0:T(8,128)(2,1)} %all-gather.15.cloned.1.call-done), kind=kOutput, calls=%fused_computation.172 | convolution fusion | flops 4927650816 | bytes 21239808 | tf_op jit(solution)/shard_map/rd,fd->rf/dot_general | solution.py:140
  381.6 6.8 convolution_convert_fusion
  388.5 9.7 convolution_convert_fusion.1
  398.3 38.6 %reduce-scatter.28.cloned.1.call-done = bf16[584,1024]{1,0:T(8,128)(2,1)} async-done(((bf16[2336,1024]{1,0:T(8,128)(2,1)}), bf16[584,1024]{1,0:T(8,128)(2,1)}) %reduce-scatter.28.cloned.1.call-update) | async-done | bytes 1196048 | tf_op jit(solution)/shard_map/reduce_scatter | solution.py:149
  440.4 47.3 %reduce-scatter.26.cloned.1.call-done = bf16[584,1024]{1,0:T(8,128)(2,1)} async-done(((bf16[2336,1024]{1,0:T(8,128)(2,1)}), bf16[584,1024]{1,0:T(8,128)(2,1)}) %reduce-scatter.26.cloned.1.call-update) | async-done | bytes 1196048 | tf_op jit(solution)/shard_map/reduce_scatter | solution.py:132
  494.6 10.0 convolution_convert_fusion.4
  508.7 9.9 fusion.92
  518.7 13.9 %all-gather.19.cloned.1.call-done = bf16[2336,1024]{1,0:T(8,128)(2,1)} async-done(((bf16[584,1024]{1,0:T(8,128)(2,1)}), bf16[2336,1024]{1,0:T(8,128)(2,1)}) %all-gather.19.cloned.1.call-update) | async-done | bytes 4784144 | tf_op jit(solution)/shard_map/all_gather | solution.py:155
  543.0 57.9 %while.29 = (s32[]{:T(128)}, f32[4,584,4,64]{1,3,2,0:T(8,128)}, bf16[4,584,4,64]{1,3,2,0:T(8,128)(2,1)}, f32[4,584,4,64]{1,3,2,0:T(8,128)}, bf16[4,584,4,64]{1,3...) while((s32[]{:T(128)}, f32[4,584,4,64]{1,3,2,0:T(8,128)}, ...), condition=%wide.region_16.17_spmd.clone, body=%wide.region_14.16_spmd.clone.sunk | while | flops 893863936 | bytes 60922828 | solution.py:188
  600.8 5.8 fusion.108
  639.4 8.9 fusion.100
  652.9 8.6 bitcast_convert_fusion
  663.4 21.4 %all-reduce = bf16[1024]{0:T(1024)(128)(2,1)S(1)} all-reduce(bf16[1024]{0:T(1024)(128)(2,1)S(1)} %get-tuple-element.332), channel_id=12, replica_groups=mesh['dp'=8,'tensor'=4] {'dp'}, use_global_device_ids=true, to_apply=%region_35.36.clone | all-reduce | flops 1024 | bytes 4096
  689.1 50.5 %reduce-scatter.40.cloned.1.call-done = bf16[32,2]{1,0:T(8,128)(2,1)} async-done(((bf16[256,2]{1,0:T(8,128)(2,1)}), bf16[32,2]{1,0:T(8,128)(2,1)}) %reduce-scatter.40.cloned.1.call-update) | async-done | bytes 144
  741.0 63.9 %reduce-scatter.42.cloned.1.call-done = bf16[128,256]{1,0:T(8,128)(2,1)} async-done(((bf16[1024,256]{1,0:T(8,128)(2,1)}), bf16[128,256]{1,0:T(8,128)(2,1)}) %reduce-scatter.42.cloned.1.call-update) | async-done | bytes 65552
  806.6 65.6 %reduce-scatter.38.cloned.1.call-done = bf16[128,768]{1,0:T(8,128)(2,1)} async-done(((bf16[1024,768]{1,0:T(8,128)(2,1)}), bf16[128,768]{1,0:T(8,128)(2,1)}) %reduce-scatter.38.cloned.1.call-update) | async-done | bytes 196624
  874.3 47.6 %reduce-scatter.30.cloned.1.call-done = bf16[584,1024]{1,0:T(8,128)(2,1)} async-done(((bf16[2336,1024]{1,0:T(8,128)(2,1)}), bf16[584,1024]{1,0:T(8,128)(2,1)}) %reduce-scatter.30.cloned.1.call-update) | async-done | bytes 1196048 | tf_op jit(solution)/shard_map/reduce_scatter | solution.py:196
  930.2 129.5 %reduce-scatter.34.cloned.1.call-done = f32[32,2]{1,0:T(8,128)} async-done(((f32[1024,2]{1,0:T(8,128)}), f32[32,2]{1,0:T(8,128)}) %reduce-scatter.34.cloned.1.call-update) | async-done | bytes 272
  1061.0 130.5 %reduce-scatter.36.cloned.1.call-done = f32[32,4]{1,0:T(8,128)} async-done(((f32[1024,4]{1,0:T(8,128)}), f32[32,4]{1,0:T(8,128)}) %reduce-scatter.36.cloned.1.call-update) | async-done | bytes 528
  (271 shorter events, 253.3 us)
Async XLA Ops:
  7.2 43.7 %copy-start = (bf16[584,1024]{1,0:T(8,128)(2,1)S(1)}, bf16[584,1024]{1,0:T(8,128)(2,1)}, u32[]{:S(2)}) copy-start(bf16[584,1024]{1,0:T(8,128)(2,1)} %param.15) | copy-start | bytes 3588100
  7.2 90.8 %all-gather.11.cloned.1.call-start = ((), (), s32[]{:S(2)}) async-start(), calls=%async_computation.12 | async-start | bytes 1769472 | tf_op jit(solution)/shard_map/all_gather | solution.py:44
  7.9 90.0 %all-gather.9.cloned.1.call-start = ((), (), s32[]{:S(2)}) async-start(), calls=%async_computation.11 | async-start | bytes 5980160 | tf_op jit(solution)/shard_map/all_gather | solution.py:69
  48.5 22.4 %copy-start.23 = (bf16[256,128]{1,0:T(8,128)(2,1)S(1)}, bf16[256,128]{1,0:T(8,128)(2,1)}, u32[]{:S(2)}) copy-start(bf16[256,128]{1,0:T(8,128)(2,1)} %param.22) | copy-start | bytes 196612
  52.5 173.0 %reduce-scatter.24.cloned.1.call-start = ((), (), s32[]{:S(2)}) async-start(), calls=%async_computation.13 | async-start | bytes 5980160 | tf_op jit(solution)/shard_map/reduce_scatter | solution.py:101
  166.8 7.4 copy-start.2
  179.1 121.7 %all-gather.13.cloned.1.call-start = ((), (), s32[]{:S(2)}) async-start(), calls=%async_computation.14 | async-start | bytes 2359296 | tf_op jit(solution)/shard_map/all_gather | solution.py:51
  179.7 148.9 %all-gather.15.cloned.1.call-start = ((), (), s32[]{:S(2)}) async-start(), calls=%async_computation.15 | async-start | bytes 2359296 | tf_op jit(solution)/shard_map/all_gather | solution.py:52
  180.3 186.4 %all-gather.17.cloned.1.call-start = ((), (), s32[]{:S(2)}) async-start(), calls=%async_computation.17 | async-start | bytes 5980160 | tf_op jit(solution)/shard_map/all_gather | solution.py:139
  230.6 206.3 %reduce-scatter.28.cloned.1.call-start = ((), (), s32[]{:S(2)}) async-start(), calls=%async_computation.18 | async-start | bytes 5980160 | tf_op jit(solution)/shard_map/reduce_scatter | solution.py:149
  230.6 35.3 %copy-start.27 = (bf16[128]{0:T(256)(128)(2,1)S(1)}, bf16[128]{0:T(256)(128)(2,1)}, u32[]{:S(2)}) copy-start(bf16[128]{0:T(256)(128)(2,1)} %param.24) | copy-start | bytes 772
  232.5 31.1 %copy-start.12 = (bf16[584,1024]{1,0:T(8,128)(2,1)}, bf16[584,1024]{1,0:T(8,128)(2,1)S(1)}, u32[]{:S(2)}) copy-start(bf16[584,1024]{1,0:T(8,128)(2,1)S(1)} %get-tuple-element.310) | copy-start | bytes 3588100
  232.5 13.9 %collective-permute-start = (bf16[584,1024]{1,0:T(8,128)(2,1)S(1)}, bf16[584,1024]{1,0:T(8,128)(2,1)S(1)}, u32[]{:S(2)}, u32[]{:S(2)}) collective-permute-start(bf16[584,1024]{1,0:T(8,128)(2,1)S(1)} %get-tuple-element.310), channel_id=1, source_target_pairs={{0,3},{1,0},{2,1},{3,2},{4,7},{5,4},{6,5},{7,6},{8,11},{9,8},{10,9... | collective-permute-start | bytes 3588104 | tf_op jit(solution)/shard_map/ppermute | solution.py:114
  247.4 16.2 %collective-permute-start.1 = (bf16[584,1024]{1,0:T(8,128)(2,1)S(1)}, bf16[584,1024]{1,0:T(8,128)(2,1)}, u32[]{:S(2)}, u32[]{:S(2)}) collective-permute-start(bf16[584,1024]{1,0:T(8,128)(2,1)S(1)} %collective-permute-done), channel_id=1, source_target_pairs={{0,3},{1,0},{2,1},{3,2},{4,7},{5,4},{6,5},{7,6},{8,11},{9,8},{10,9... | collective-permute-start | bytes 3588104 | tf_op jit(solution)/shard_map/ppermute | solution.py:114
  263.6 27.6 %collective-permute-start.2 = (bf16[584,1024]{1,0:T(8,128)(2,1)}, bf16[584,1024]{1,0:T(8,128)(2,1)}, u32[]{:S(2)}, u32[]{:S(2)}) collective-permute-start(bf16[584,1024]{1,0:T(8,128)(2,1)} %collective-permute-done.1), channel_id=1, source_target_pairs={{0,3},{1,0},{2,1},{3,2},{4,7},{5,4},{6,5},{7,6},{8,11},{9,8},{10,9... | collective-permute-start | bytes 3588104 | tf_op jit(solution)/shard_map/ppermute | solution.py:114
  288.7 5.0 copy-start.13
  366.8 14.8 %copy-start.28 = (bf16[1024,1024]{1,0:T(8,128)(2,1)S(1)}, bf16[1024,1024]{1,0:T(8,128)(2,1)}, u32[]{:S(2)}) copy-start(bf16[1024,1024]{1,0:T(8,128)(2,1)} %all-gather.13.cloned.1.call-done) | copy-start | bytes 6291460
  388.4 99.3 %reduce-scatter.26.cloned.1.call-start = ((), (), s32[]{:S(2)}) async-start(), calls=%async_computation.16 | async-start | bytes 5980160 | tf_op jit(solution)/shard_map/reduce_scatter | solution.py:132
  398.2 89.5 %copy-start.24 = (f32[1,1024]{1,0:T(1,128)S(1)}, f32[1,1024]{1,0:T(1,128)}, u32[]{:S(2)}) copy-start(f32[1,1024]{1,0:T(1,128)} %get-tuple-element.322) | copy-start | bytes 12292
  398.2 134.3 %all-gather.19.cloned.1.call-start = ((), (), s32[]{:S(2)}) async-start(), calls=%async_computation.19 | async-start | bytes 5980160 | tf_op jit(solution)/shard_map/all_gather | solution.py:155
  494.6 190.8 %reduce-scatter.44.cloned.1.call-start = ((), (), s32[]{:S(2)}) async-start(), calls=%async_computation.27 | async-start | bytes 2359296
  508.6 178.7 %reduce-scatter.32.cloned.1.call-start = ((), (), s32[]{:S(2)}) async-start(), calls=%async_computation.21 | async-start | bytes 2359296 | tf_op jit(solution)/shard_map/reduce_scatter | solution.py:221
  518.6 221.0 %reduce-scatter.40.cloned.1.call-start = ((), (), s32[]{:S(2)}) async-start(), calls=%async_computation.25 | async-start | bytes 73728
  617.6 7.2 copy-start.5
  624.7 180.3 %reduce-scatter.42.cloned.1.call-start = ((), (), s32[]{:S(2)}) async-start(), calls=%async_computation.26 | async-start | bytes 589824
  638.2 233.9 %reduce-scatter.38.cloned.1.call-start = ((), (), s32[]{:S(2)}) async-start(), calls=%async_computation.24 | async-start | bytes 1769472
  652.9 269.0 %reduce-scatter.30.cloned.1.call-start = ((), (), s32[]{:S(2)}) async-start(), calls=%async_computation.20 | async-start | bytes 5980160 | tf_op jit(solution)/shard_map/reduce_scatter | solution.py:196
  661.6 260.3 %copy-start.18 = (f32[584]{0:T(1024)S(1)}, f32[584]{0:T(1024)}, u32[]{:S(2)}) copy-start(f32[584]{0:T(1024)} %copy-done.17) | copy-start | bytes 7012
  661.6 260.3 %copy-start.20 = (f32[584]{0:T(1024)S(1)}, f32[584]{0:T(1024)}, u32[]{:S(2)}) copy-start(f32[584]{0:T(1024)} %copy-done.19) | copy-start | bytes 7012
  661.6 260.3 %copy-start.22 = (f32[1,1024]{1,0:T(1,128)S(1)}, f32[1,1024]{1,0:T(1,128)}, u32[]{:S(2)}) copy-start(f32[1,1024]{1,0:T(1,128)} %copy-done.21) | copy-start | bytes 12292
  661.6 398.1 %reduce-scatter.34.cloned.1.call-start = ((), (), s32[]{:S(2)}) async-start(), calls=%async_computation.22 | async-start | bytes 540672
  925.5 266.1 %reduce-scatter.36.cloned.1.call-start = ((), (), s32[]{:S(2)}) async-start(), calls=%async_computation.23 | async-start | bytes 540672
  (28 other events, 63.2 us)
Sparse Core Ops, SparseCore 0:
  10.2 46.6 all-gather.10
  59.1 36.6 all-gather.8
  179.3 46.1 reduce-scatter.23
  227.6 49.2 all-gather.12
  279.0 49.5 all-gather.14
  330.7 35.9 all-gather.16
  388.6 48.2 reduce-scatter.27
  439.4 48.2 reduce-scatter.25
  494.7 37.8 all-gather.18
  536.4 67.9 reduce-scatter.43
  608.3 66.8 reduce-scatter.31
  679.4 60.1 reduce-scatter.39
  743.9 60.9 reduce-scatter.41
  808.2 63.8 reduce-scatter.37
  874.7 47.1 reduce-scatter.29
  925.6 134.0 reduce-scatter.33
  1061.9 129.6 reduce-scatter.35
